TPU v7x, 128 devices: a whole 4x4x4 slice. The times are simulated.
128 devices in a mesh: outer: 4 (over x), ctr: 32 (over y, z, core).
Axes of the slice: x: 4, y: 4, z: 4, core: 2. Of those that a mesh axis runs over, the one named last changes fastest.
Arguments:
- amplitudes: float32 [1024, 131072], P(('outer', 'ctr')), may hold values from -24 to 24
- integrals: float32 [4096, 131072], P('outer', 'ctr'), may hold values from -0.015625 to 0.015625
- block_mask: int32 [32, 1024], P('outer', 'ctr'), may hold values 0 or 1
Outputs:
- ladder: float32 [1024, 4096], P('ctr', 'outer')
All inputs are finite; a program needn't handle non-finite values. No bound on the sum of `block_mask` on one device may be relied on, other than what follows from the above.
Results may differ from a plain program's by a relative error of at most 0.000071.
Values sent between devices are 32-bit elements; how exact they have to be, the bound alone decides.
A program may use at most 128 MiB of HBM per device.

v0:
```python
import jax
import jax.numpy as jnp
from jax import lax
from jax.sharding import PartitionSpec as P


def local(amplitudes, integrals, block_mask):
    ab_rows = integrals.shape[0]
    cd_cols = integrals.shape[1]
    ab_blocks = block_mask.shape[0]
    cd_blocks = block_mask.shape[1]
    tile_rows = ab_rows // ab_blocks
    tile_cols = cd_cols // cd_blocks
    mask_f = block_mask.astype(jnp.float32)
    shaped = integrals.reshape(ab_blocks, tile_rows, cd_blocks, tile_cols)
    sparse_v = (shaped * mask_f[:, None, :, None]).reshape(ab_rows, cd_cols)
    local_rows = lax.all_to_all(amplitudes, "ctr", split_axis=1, concat_axis=0, tiled=True)
    partial_terms = lax.dot_general(
        lax.all_gather(local_rows, "outer", axis=0, tiled=True),
        sparse_v,
        (((1,), (1,)), ((), ())),
        precision=lax.Precision.HIGHEST,
        preferred_element_type=jnp.float32,
    )
    summed = lax.psum(partial_terms, "ctr")
    own_rows = summed.shape[0] // lax.axis_size("ctr")
    offset = lax.axis_index("ctr") * own_rows
    result = lax.dynamic_slice_in_dim(summed, offset, own_rows, 0)
    return result


def solution(mesh):
    return jax.shard_map(
        local,
        mesh=mesh,
        in_specs=(P(("outer", "ctr"), None), P("outer", "ctr"), P("outer", "ctr")),
        out_specs=P("ctr", "outer"),
        check_vma=False,
    )
```

profile of v0, /device:TPU:2, one launch (start us, length us, event | category | flops | bytes accessed | tf_op | source)
XLA Modules:
  0.0 414.4 jit_solution(17326440921595013472)
XLA Ops:
  6.5 0.0 all-gather.2.cloned.1.call-start
  6.5 58.9 %all_to_all.19 = f32[8,32,4096]{2,0,1:T(8,128)} all-to-all(f32[8,32,4096]{2,0,1:T(8,128)} %bitcast.20), channel_id=1, replica_groups=mesh['outer'=4,'ctr'=32] {'ctr'}, dimensions={1} | all-to-all | bytes 8388608 | tf_op jit(solution)/shard_map/all_to_all | solution.py:17
  65.5 0.0 all-gather.2.cloned.1.call-update
  65.5 0.0 all-reduce.2.cloned.1.call-start
  65.5 0.7 convert_element_type.3
  66.2 151.5 %all-gather.2.cloned.1.call-done = f32[1024,4096]{1,0:T(8,128)} async-done(((f32[256,4096]{1,0:T(8,128)}), f32[1024,4096]{1,0:T(8,128)}) %all-gather.2.cloned.1.call-update) | async-done | bytes 16777232 | tf_op jit(solution)/shard_map/all_gather | solution.py:19
  217.7 2.2 mul.14
  219.9 72.8 %fusion.2 = f32[1024,1024]{0,1:T(8,128)} fusion(f32[1024,4096]{1,0:T(8,128)} %all-gather.2.cloned.1.call-done, f32[1024,4096]{1,0:T(8,128)} %param.4, f32[128,8,32,128]{3,2,1,0:T(8,128)S(1)} %bitcast.18), kind=kOutput, calls=%fused_computation.3 | convolution fusion | flops 51543801856 | bytes 54525952 | tf_op jit(solution)/shard_map/dot_general | solution.py:18
  292.7 0.0 all-reduce.2.cloned.1.call-update
  292.8 112.8 %all-reduce.2.cloned.1.call-done = f32[1024,1024]{0,1:T(8,128)} async-done(((f32[1024,1024]{0,1:T(8,128)}), f32[1024,1024]{0,1:T(8,128)}) %all-reduce.2.cloned.1.call-update) | async-done | bytes 4194320 | tf_op jit(solution)/shard_map/psum | solution.py:25
  405.5 1.2 constant_dynamic-slice_fusion
  406.8 0.8 copy.4
Async XLA Ops:
  6.5 211.2 %all-gather.2.cloned.1.call-start = ((), (), s32[]{:S(2)}) async-start(), calls=%async_computation.1 | async-start | bytes 20971520 | tf_op jit(solution)/shard_map/all_gather | solution.py:19
  65.5 340.0 %all-reduce.2.cloned.1.call-start = ((), (), s32[]{:S(2)}) async-start(), calls=%async_computation.2 | async-start | bytes 8388608 | tf_op jit(solution)/shard_map/psum | solution.py:25
Sparse Core Ops, SparseCore 0:
  65.6 152.0 all-gather.1
  292.9 112.6 all-reduce.1
where the time goes:
time: 416 us; the launch traced here: 414 us
  waiting for transfers between devices  264 us (63%)
  matrix products  72.8 us (18%)
  blocking collectives  58.9 us (14%)
  between operations  13.4 us (3%)
  local copies, waits for them, and re-layouts  4.28 us (1%)
    all_gather x1, waiting for transfers between devices, local(): lax.all_gather(local_rows, 'outer', axis=0, tiled=True)  151 us
    psum x1, waiting for transfers between devices, local(): summed = lax.psum(partial_terms, 'ctr')  113 us
    dot_general x1, matrix products, local(): lax.dot_general(lax.all_gather(local_rows, 'outer', axis=0, tiled=True),...  72.8 us
    all_to_all x1, blocking collectives, local(): lax.all_to_all(amplitudes, 'ctr', split_axis=1, concat_axis=0, tiled=True)  58.9 us
  transfers between devices with their start and end apart: 2, of which 2 were waited for; matrix products, arithmetic and copies ran while one was open for 0% of the time, Pallas kernels for 0%

commit v1 on v0

v1 whole, which is shorter than its diff:
```python
import functools

import jax
import jax.numpy as jnp
from jax import lax
from jax.experimental import pallas as pl
from jax.experimental.pallas import tpu as pltpu
from jax.sharding import PartitionSpec as P

MESH = pl.DeviceIdType.MESH
F32 = jnp.float32
BF16 = jnp.bfloat16
ROWS = 8
COLS = 4096
TILE = 128
AB = 1024
CHUNKS = 8
QUART = COLS // 4
UNITS = 4 * CHUNKS
AHEAD = 3
LAG = 7
NT = 256


def body(amp, integ, mask, out, t, vhi, vlo, stage, acc, land, own_sem, v_sem,
         a_send, a_recv, d_send, d_recv, f_send, f_recv, r_send, r_recv):
    o = lax.axis_index("outer")
    c = lax.axis_index("ctr")
    y = c // 8
    z = lax.rem(c // 2, 4)
    k = lax.rem(c, 2)
    right = lax.rem(o + 1, 4)
    left = lax.rem(o + 3, 4)

    def v_copy(v):
        return pltpu.make_async_copy(
            integ.at[pl.ds(v * TILE, TILE), :], stage.at[v % 2], v_sem.at[v % 2])

    v_copy(0).start()
    v_copy(1).start()

    barrier = pltpu.get_barrier_semaphore()
    for i in range(1, 32):
        pl.semaphore_signal(barrier, inc=1, device_id={"outer": o, "ctr": lax.rem(c + i, 32)}, device_id_type=MESH)
    for x in (right, left):
        pl.semaphore_signal(barrier, inc=1, device_id={"outer": x, "ctr": c}, device_id_type=MESH)
    pl.semaphore_wait(barrier, 33)

    def cols_of(ctr):
        return pl.ds(pl.multiple_of(ctr * COLS, COLS), COLS)

    def a_copy(q, core):
        to = lax.rem(y + 4 - q // 4, 4) * 8 + lax.rem(z + 4 - lax.rem(q, 4), 4) * 2 + core
        return pltpu.make_async_remote_copy(
            src_ref=amp.at[:, cols_of(to)],
            dst_ref=t.at[q // 2, 0, lax.rem(q, 2) * 2 + k],
            send_sem=a_send.at[2 * q + core],
            recv_sem=a_recv.at[2 * q + k],
            device_id={"outer": o, "ctr": to}, device_id_type=MESH)

    def a_wait(slot):
        pltpu.make_async_copy(
            t.at[0, 0, 0], t.at[slot // 4, 0, lax.rem(slot, 4)], a_recv.at[slot]).wait()

    own = pltpu.make_async_copy(amp.at[:, cols_of(c)], t.at[0, 0, k], own_sem)
    own.start()

    def x_copy(src, dst, sems, recvs, u, d):
        return pltpu.make_async_remote_copy(
            src_ref=src, dst_ref=dst, send_sem=sems.at[u, d], recv_sem=recvs.at[u, d],
            device_id={"outer": (right, left)[d], "ctr": c}, device_id_type=MESH)

    def quart(u):
        return pl.ds(pl.multiple_of(lax.rem(u, 4) * QUART, QUART), QUART)

    def direct(u, d, first=False):
        if first:
            slot = k if u == 0 else 1 - k if u == 1 else u
            src = amp.at[:, cols_of(c)] if u == 0 else t.at[0, 0, slot]
            return x_copy(src, t.at[0, (3, 1)[d], slot], d_send, d_recv, u, d)
        ch = u // 4
        return x_copy(t.at[ch, 0, :, :, quart(u)], t.at[ch, (3, 1)[d], :, :, quart(u)], d_send, d_recv, u, d)

    def forward(u, d, first=False):
        if first:
            slot = k if u == 0 else 1 - k if u == 1 else u
            half = pl.ds(d * (COLS // 2), COLS // 2)
            return x_copy(t.at[0, (3, 1)[d], slot, :, half], t.at[0, 2, slot, :, half], f_send, f_recv, u, d)
        ch = u // 4
        two = pl.ds(2 * d, 2)
        return x_copy(t.at[ch, (3, 1)[d], two, :, quart(u)], t.at[ch, 2, two, :, quart(u)], f_send, f_recv, u, d)

    def vprep(v):
        v_copy(v).wait()

        @pl.loop(0, COLS // TILE)
        def _(b):
            at = pl.ds(pl.multiple_of(b * TILE, TILE), TILE)
            m = mask[v, b].astype(F32)
            x = stage[v % 2, :, at] * m
            hi = x.astype(BF16)
            lo = (x - hi.astype(F32)).astype(BF16)
            vhi[pl.ds(v * TILE, TILE), at] = hi
            vlo[pl.ds(v * TILE, TILE), at] = lo

        if v + 2 < AB // TILE:
            v_copy(v + 2).start()

    def multiply(u):
        ch = u // 4
        rows = t[ch, :, :, :, quart(u)].reshape(4 * 4 * ROWS, QUART)
        hi = rows.astype(BF16)
        lo = (rows - hi.astype(F32)).astype(BF16)
        both = jnp.concatenate([hi, lo], axis=0)
        dims = (((1,), (1,)), ((), ()))

        @pl.loop(0, AB // NT)
        def _(n):
            at = pl.ds(pl.multiple_of(n * NT, NT), NT)
            a = lax.dot_general(both, vhi[at, quart(u)], dims, preferred_element_type=F32)
            b = lax.dot_general(hi, vlo[at, quart(u)], dims, preferred_element_type=F32)
            p = a[:128] + a[128:] + b
            p = p.reshape(16, ROWS, NT)

            @pl.when(lax.rem(u, 4) == 0)
            def _():
                acc[ch, :, :, at] = p

            @pl.when(lax.rem(u, 4) != 0)
            def _():
                acc[ch, :, :, at] += p

    def spread(ch, p, h):
        q = 2 * ch + h
        ys = lax.rem(y + q // 4, 4)
        zs = lax.rem(z + lax.rem(q, 4), 4)
        to = 8 * lax.rem(o + p, 4) + 2 * ys + zs // 2
        src = acc.at[ch, pl.ds(4 * p + 2 * h, 2)]
        dst = land.at[c, pl.ds(2 * lax.rem(zs, 2), 2)]
        sem = r_send.at[8 * ch + 2 * p + h]
        return to, lax.rem(zs, 2), src, dst, sem

    def spread_start(ch):
        @pl.loop(0, 8)
        def _(i):
            to, b, src, dst, sem = spread(ch, i // 2, lax.rem(i, 2))

            @pl.when(to == c)
            def _():
                pltpu.make_async_copy(src, dst, sem).start()

            @pl.when(to != c)
            def _():
                pltpu.make_async_remote_copy(
                    src_ref=src, dst_ref=dst, send_sem=sem, recv_sem=r_recv.at[2 * c + b],
                    device_id={"outer": o, "ctr": to}, device_id_type=MESH).start()

    a_copy(0, 1 - k).start()
    for d in (0, 1):
        direct(0, d, True).start()

    @pl.loop(2, 32)
    def _(i):
        a_copy(i // 2, lax.rem(i, 2)).start()

    a_wait(1 - k)
    for d in (0, 1):
        direct(1, d, True).start()
    vprep(0)
    a_wait(2)
    for d in (0, 1):
        direct(2, d, True).start()

    for s in range(LAG):
        u = s + AHEAD
        if u < 4:
            a_wait(u)
            for d in (0, 1):
                direct(u, d, True).start()
        else:
            if u % 4 == 0:
                for j in range(4):
                    a_wait(u + j)
            for d in (0, 1):
                direct(u, d).start()
        for d in (0, 1):
            direct(s, d, s < 4).wait_recv()
            forward(s, d, s < 4).start()
        vprep(s + 1)
        if s >= 4:
            for d in (0, 1):
                forward(s - 4, d, s < 8).wait_recv()
    own.wait()

    @pl.loop(LAG, UNITS + LAG)
    def _(s):
        @pl.when(s < UNITS - AHEAD)
        def _():
            u = s + AHEAD

            @pl.when(lax.rem(u, 4) == 0)
            def _():
                for j in range(4):
                    a_wait(u + j)
            for d in (0, 1):
                direct(u, d).start()

        @pl.when(s < UNITS)
        def _():
            for d in (0, 1):
                direct(s, d).wait_recv()
                forward(s, d).start()

        @pl.when(s == LAG)
        def _():
            for d in (0, 1):
                forward(3, d, True).wait_recv()

        @pl.when((s > LAG) & (s < UNITS))
        def _():
            for d in (0, 1):
                forward(s - 4, d).wait_recv()

        @pl.when(s >= UNITS + LAG - 4)
        def _():
            for d in (0, 1):
                forward(s - LAG, d).wait_recv()
        u = s - LAG
        multiply(u)

        @pl.when(lax.rem(u, 4) == 3)
        def _():
            spread_start(u // 4)

    a_copy(0, 1 - k).wait_send()

    @pl.loop(2, 32)
    def _(i):
        a_copy(i // 2, lax.rem(i, 2)).wait_send()
    for u in range(4):
        for d in (0, 1):
            direct(u, d, True).wait_send()
            forward(u, d, True).wait_send()

    @pl.loop(4, UNITS)
    def _(u):
        for d in (0, 1):
            direct(u, d).wait_send()
            forward(u, d).wait_send()

    @pl.loop(0, 64)
    def _(i):
        _, _, src, dst, sem = spread(i // 8, lax.rem(i // 2, 4), lax.rem(i, 2))
        pltpu.make_async_copy(src, dst, sem).wait()

    @pl.loop(0, 64)
    def _(i):
        @pl.when(i // 2 != c)
        def _():
            piece = land.at[i // 2, pl.ds(2 * lax.rem(i, 2), 2)]
            pltpu.make_async_copy(piece, piece, r_recv.at[i]).wait()

    @pl.loop(0, 4)
    def _(r):
        total = land[0, r]
        for i in range(1, 32):
            total = total + land[i, r]
        out[pl.ds(pl.multiple_of(r * ROWS, ROWS), ROWS), :] = total


def local(amplitudes, integrals, block_mask):
    dma = pltpu.SemaphoreType.DMA
    return pl.pallas_call(
        body,
        name="ladder",
        out_shape=jax.ShapeDtypeStruct((4 * ROWS, AB), F32),
        in_specs=[
            pl.BlockSpec(memory_space=pl.ANY),
            pl.BlockSpec(memory_space=pl.ANY),
            pl.BlockSpec(memory_space=pltpu.SMEM),
        ],
        out_specs=pl.BlockSpec(memory_space=pltpu.VMEM),
        scratch_shapes=[
            pltpu.VMEM((CHUNKS, 4, 4, ROWS, COLS), F32),
            pltpu.VMEM((AB, COLS), BF16),
            pltpu.VMEM((AB, COLS), BF16),
            pltpu.VMEM((2, TILE, COLS), F32),
            pltpu.VMEM((CHUNKS, 16, ROWS, AB), F32),
            pltpu.VMEM((32, 4, ROWS, AB), F32),
            dma,
            dma((2,)),
            dma((32,)), dma((32,)),
            dma((UNITS, 2)), dma((UNITS, 2)),
            dma((UNITS, 2)), dma((UNITS, 2)),
            dma((64,)), dma((64,)),
        ],
        compiler_params=pltpu.CompilerParams(
            collective_id=0, has_side_effects=True, vmem_limit_bytes=64 * 2**20 - 65536),
    )(amplitudes, integrals, block_mask)


def solution(mesh):
    return jax.shard_map(
        local,
        mesh=mesh,
        in_specs=(P(("outer", "ctr"), None), P("outer", "ctr"), P("outer", "ctr")),
        out_specs=P("ctr", "outer"),
        check_vma=False,
    )
```

time: 416 us -> 204 us (0.49)
  the two profiles are of different devices: /device:TPU:2 before, /device:TPU:35 now
where the time goes in v1:
time: 204 us
  Pallas kernels  202 us (99%)
    pallas_call x1, Pallas kernels, local(): pl.pallas_call(body, name='ladder', out_shape=jax.ShapeDtypeStruct((4 * R...  202 us

profile of v1, /device:TPU:35, one launch (start us, length us, event | category | flops | bytes accessed | tf_op | source)
XLA Modules:
  0.0 203.7 jit_solution(8053138901988162149)
XLA Ops:
  0.0 202.1 %ladder.1 = f32[32,1024]{1,0:T(8,128)} custom-call(f32[8,131072]{1,0:T(8,128)} %amp.1, f32[1024,4096]{1,0:T(8,128)} %integ.1, s32[8,32]{1,0:T(8,128)} %mask.1), custom_call_target="tpu_custom_call" | custom-call | tf_op jit(solution)/shard_map/ladder/pallas_call | solution.py:273
  202.1 1.6 copy.5

commit v2 on v1

--- a/solution.py
+++ b/solution.py
@@ -22,6 +22,20 @@
 NT = 256
 
 
+ORDER = ((0, 0), (0, 1), (0, 3), (1, 0), (3, 0), (1, 1), (3, 3), (1, 3),
+         (3, 1), (0, 2), (2, 0), (1, 2), (3, 2), (2, 1), (2, 3), (2, 2))
+DY = [a for a, _ in ORDER]
+DZ = [b for _, b in ORDER]
+
+
+def packed(table, q):
+    if isinstance(q, int):
+        return table[q]
+    word = sum(value << (2 * i) for i, value in enumerate(table))
+    word = word - 2**32 if word >= 2**31 else word
+    return lax.bitwise_and(lax.shift_right_logical(jnp.int32(word), 2 * q), jnp.int32(3))
+
+
 def body(amp, integ, mask, out, t, vhi, vlo, stage, acc, land, own_sem, v_sem,
          a_send, a_recv, d_send, d_recv, f_send, f_recv, r_send, r_recv):
     o = lax.axis_index("outer")
@@ -49,8 +63,12 @@
     def cols_of(ctr):
         return pl.ds(pl.multiple_of(ctr * COLS, COLS), COLS)
 
+    def offset(q):
+        return packed(DY, q), packed(DZ, q)
+
     def a_copy(q, core):
-        to = lax.rem(y + 4 - q // 4, 4) * 8 + lax.rem(z + 4 - lax.rem(q, 4), 4) * 2 + core
+        dy, dz = offset(q)
+        to = lax.rem(y + 4 - dy, 4) * 8 + lax.rem(z + 4 - dz, 4) * 2 + core
         return pltpu.make_async_remote_copy(
             src_ref=amp.at[:, cols_of(to)],
             dst_ref=t.at[q // 2, 0, lax.rem(q, 2) * 2 + k],
@@ -132,8 +150,9 @@
 
     def spread(ch, p, h):
         q = 2 * ch + h
-        ys = lax.rem(y + q // 4, 4)
-        zs = lax.rem(z + lax.rem(q, 4), 4)
+        dy, dz = offset(q)
+        ys = lax.rem(y + dy, 4)
+        zs = lax.rem(z + dz, 4)
         to = 8 * lax.rem(o + p, 4) + 2 * ys + zs // 2
         src = acc.at[ch, pl.ds(4 * p + 2 * h, 2)]
         dst = land.at[c, pl.ds(2 * lax.rem(zs, 2), 2)]
@@ -159,9 +178,12 @@
     for d in (0, 1):
         direct(0, d, True).start()
 
-    @pl.loop(2, 32)
-    def _(i):
-        a_copy(i // 2, lax.rem(i, 2)).start()
+    def a_start(ch):
+        for i in range(4):
+            a_copy(2 * ch + i // 2, i % 2).start()
+
+    for i in range(2, 10):
+        a_copy(i // 2, i % 2).start()
 
     a_wait(1 - k)
     for d in (0, 1):
@@ -173,6 +195,11 @@
 
     for s in range(LAG):
         u = s + AHEAD
+        if s == 0:
+            for i in range(10, 12):
+                a_copy(i // 2, i % 2).start()
+        if s % 4 == 0 and s:
+            a_start(s // 4 + 2)
         if u < 4:
             a_wait(u)
             for d in (0, 1):
@@ -194,6 +221,10 @@
 
     @pl.loop(LAG, UNITS + LAG)
     def _(s):
+        @pl.when((lax.rem(s, 4) == 0) & (s <= 4 * (CHUNKS - 3)))
+        def _():
+            a_start(s // 4 + 2)
+
         @pl.when(s < UNITS - AHEAD)
         def _():
             u = s + AHEAD

time: 204 us -> 173 us (0.85)
  the two profiles are of different devices: /device:TPU:35 before, /device:TPU:2 now
where the time goes in v2:
time: 173 us
  Pallas kernels  172 us (99%)
    pallas_call x1, Pallas kernels, local(): pl.pallas_call(body, name='ladder', out_shape=jax.ShapeDtypeStruct((4 * R...  172 us

profile of v2, /device:TPU:2, one launch (start us, length us, event | category | flops | bytes accessed | tf_op | source)
XLA Modules:
  0.0 173.3 jit_solution(3229040891273338570)
XLA Ops:
  0.0 171.8 %ladder.1 = f32[32,1024]{1,0:T(8,128)} custom-call(f32[8,131072]{1,0:T(8,128)} %amp.1, f32[1024,4096]{1,0:T(8,128)} %integ.1, s32[8,32]{1,0:T(8,128)} %mask.1), custom_call_target="tpu_custom_call" | custom-call | tf_op jit(solution)/shard_map/ladder/pallas_call | solution.py:304
  171.8 1.6 copy.5

commit v3 on v2

--- a/solution.py
+++ b/solution.py
@@ -18,7 +18,8 @@
 QUART = COLS // 4
 UNITS = 4 * CHUNKS
 AHEAD = 3
-LAG = 7
+START = 7
+LAG = 4
 NT = 256
 
 
@@ -188,18 +189,20 @@
     a_wait(1 - k)
     for d in (0, 1):
         direct(1, d, True).start()
-    vprep(0)
     a_wait(2)
     for d in (0, 1):
         direct(2, d, True).start()
 
-    for s in range(LAG):
+    for s in range(START):
         u = s + AHEAD
         if s == 0:
             for i in range(10, 12):
                 a_copy(i // 2, i % 2).start()
         if s % 4 == 0 and s:
             a_start(s // 4 + 2)
+        for d in (0, 1):
+            direct(s, d, s < 4).wait_recv()
+            forward(s, d, s < 4).start()
         if u < 4:
             a_wait(u)
             for d in (0, 1):
@@ -210,21 +213,25 @@
                     a_wait(u + j)
             for d in (0, 1):
                 direct(u, d).start()
-        for d in (0, 1):
-            direct(s, d, s < 4).wait_recv()
-            forward(s, d, s < 4).start()
-        vprep(s + 1)
+        vprep(s)
         if s >= 4:
             for d in (0, 1):
                 forward(s - 4, d, s < 8).wait_recv()
     own.wait()
-
-    @pl.loop(LAG, UNITS + LAG)
+    vprep(START)
+
+    @pl.loop(START, UNITS + LAG)
     def _(s):
         @pl.when((lax.rem(s, 4) == 0) & (s <= 4 * (CHUNKS - 3)))
         def _():
             a_start(s // 4 + 2)
 
+        @pl.when(s < UNITS)
+        def _():
+            for d in (0, 1):
+                direct(s, d).wait_recv()
+                forward(s, d).start()
+
         @pl.when(s < UNITS - AHEAD)
         def _():
             u = s + AHEAD
@@ -236,32 +243,26 @@
             for d in (0, 1):
                 direct(u, d).start()
 
-        @pl.when(s < UNITS)
-        def _():
-            for d in (0, 1):
-                direct(s, d).wait_recv()
-                forward(s, d).start()
-
-        @pl.when(s == LAG)
-        def _():
-            for d in (0, 1):
-                forward(3, d, True).wait_recv()
-
-        @pl.when((s > LAG) & (s < UNITS))
-        def _():
-            for d in (0, 1):
-                forward(s - 4, d).wait_recv()
-
-        @pl.when(s >= UNITS + LAG - 4)
+        @pl.when(s == START)
+        def _():
+            for d in (0, 1):
+                forward(START - LAG, d, True).wait_recv()
+
+        @pl.when(s > START)
         def _():
             for d in (0, 1):
                 forward(s - LAG, d).wait_recv()
-        u = s - LAG
-        multiply(u)
-
-        @pl.when(lax.rem(u, 4) == 3)
-        def _():
-            spread_start(u // 4)
+
+        first = jnp.minimum(2 * (s - START), s - LAG)
+        last = jnp.minimum(2 * (s - START) + 2, s - LAG + 1)
+
+        @pl.loop(first, last)
+        def _(u):
+            multiply(u)
+
+            @pl.when(lax.rem(u, 4) == 3)
+            def _():
+                spread_start(u // 4)
 
     a_copy(0, 1 - k).wait_send()
 

time: 173 us -> 169 us (0.977)
  Pallas kernels: 172 us -> 167 us
    pallas_call x1, Pallas kernels: 172 us -> 167 us  [local(): pl.pallas_call(body, name='ladder', out_shape=jax.ShapeDtypeStruct((4 * R...]
where the time goes in v3:
time: 169 us
  Pallas kernels  167 us (99%)
    pallas_call x1, Pallas kernels, local(): pl.pallas_call(body, name='ladder', out_shape=jax.ShapeDtypeStruct((4 * R...  167 us

profile of v3, /device:TPU:2, one launch (start us, length us, event | category | flops | bytes accessed | tf_op | source)
XLA Modules:
  0.0 168.7 jit_solution(11789666503495212262)
XLA Ops:
  0.0 167.2 %ladder.1 = f32[32,1024]{1,0:T(8,128)} custom-call(f32[8,131072]{1,0:T(8,128)} %amp.1, f32[1024,4096]{1,0:T(8,128)} %integ.1, s32[8,32]{1,0:T(8,128)} %mask.1), custom_call_target="tpu_custom_call" | custom-call | tf_op jit(solution)/shard_map/ladder/pallas_call | solution.py:305
  167.2 1.6 copy.5

commit v4 on v3

--- a/solution.py
+++ b/solution.py
@@ -189,6 +189,7 @@
     a_wait(1 - k)
     for d in (0, 1):
         direct(1, d, True).start()
+    vprep(0)
     a_wait(2)
     for d in (0, 1):
         direct(2, d, True).start()
@@ -200,9 +201,6 @@
                 a_copy(i // 2, i % 2).start()
         if s % 4 == 0 and s:
             a_start(s // 4 + 2)
-        for d in (0, 1):
-            direct(s, d, s < 4).wait_recv()
-            forward(s, d, s < 4).start()
         if u < 4:
             a_wait(u)
             for d in (0, 1):
@@ -213,12 +211,14 @@
                     a_wait(u + j)
             for d in (0, 1):
                 direct(u, d).start()
-        vprep(s)
+        for d in (0, 1):
+            direct(s, d, s < 4).wait_recv()
+            forward(s, d, s < 4).start()
+        vprep(s + 1)
         if s >= 4:
             for d in (0, 1):
                 forward(s - 4, d, s < 8).wait_recv()
     own.wait()
-    vprep(START)
 
     @pl.loop(START, UNITS + LAG)
     def _(s):
@@ -226,22 +226,22 @@
         def _():
             a_start(s // 4 + 2)
 
+        @pl.when(s < UNITS - AHEAD)
+        def _():
+            u = s + AHEAD
+
+            @pl.when(lax.rem(u, 4) == 0)
+            def _():
+                for j in range(4):
+                    a_wait(u + j)
+            for d in (0, 1):
+                direct(u, d).start()
+
         @pl.when(s < UNITS)
         def _():
             for d in (0, 1):
                 direct(s, d).wait_recv()
                 forward(s, d).start()
-
-        @pl.when(s < UNITS - AHEAD)
-        def _():
-            u = s + AHEAD
-
-            @pl.when(lax.rem(u, 4) == 0)
-            def _():
-                for j in range(4):
-                    a_wait(u + j)
-            for d in (0, 1):
-                direct(u, d).start()
 
         @pl.when(s == START)
         def _():

time: 169 us -> 167 us (0.988)
  no operation moved by 1% of the time
where the time goes in v4:
time: 167 us
  Pallas kernels  166 us (99%)
    pallas_call x1, Pallas kernels, local(): pl.pallas_call(body, name='ladder', out_shape=jax.ShapeDtypeStruct((4 * R...  166 us

profile of v4, /device:TPU:2, one launch (start us, length us, event | category | flops | bytes accessed | tf_op | source)
XLA Modules:
  0.0 167.3 jit_solution(4046170437999343310)
XLA Ops:
  0.0 165.7 %ladder.1 = f32[32,1024]{1,0:T(8,128)} custom-call(f32[8,131072]{1,0:T(8,128)} %amp.1, f32[1024,4096]{1,0:T(8,128)} %integ.1, s32[8,32]{1,0:T(8,128)} %mask.1), custom_call_target="tpu_custom_call" | custom-call | tf_op jit(solution)/shard_map/ladder/pallas_call | solution.py:305
  165.8 1.6 copy.5
